TPU v7x, 512 devices: a whole 4x4x16 slice. The times are simulated.
512 devices in a mesh: leaf: 32 (over x, y, core), row: 16 (over z).
Axes of the slice: x: 4, y: 4, z: 16, core: 2. Of those that a mesh axis runs over, the one named last changes fastest.
Arguments:
- rhs: bfloat16 [32, 16, 189, 512], P('leaf', 'row'), may hold values from -6 to 6
- inv_diag: bfloat16 [32, 16, 189, 1536], P('leaf', 'row'), may hold values from -0.15625 to 0.15625
- off_diag: bfloat16 [32, 16, 96, 12384], P('leaf', 'row'), may hold values from -0.0390625 to 0.0390625
- pair_mask: int32 [32, 16, 15], P('leaf', 'row'), may hold values 0 or 1
Outputs:
- solution: float32 [32, 16, 189, 512], P('leaf', 'row')
All inputs are finite; a program needn't handle non-finite values. No bound on the sum of `pair_mask` on one device may be relied on, other than what follows from the above.
Results may differ from a plain program's by a relative error of at most 0.0065.
Values may be sent and summed in bfloat16 or wider, within the bound.
No kernel may reach another device: no remote copies, remote signals or barrier semaphores. Data moves between devices by JAX's collectives and lax.ppermute only.
A program may use at most 64 MiB of HBM per device.

v0:
```python
import jax
import jax.numpy as jnp
from jax import lax
from jax.sharding import PartitionSpec as P

F32 = jnp.float32
BF16 = jnp.bfloat16


def column_start(ancestor, source, width_all):
    offset = 0
    for higher in range(1, ancestor):
        for within in range(higher):
            offset += width_all // 2**within
    for within in range(source):
        offset += width_all // 2**within
    return offset


def dot(a, b):
    return jnp.dot(a, b, preferred_element_type=F32)


def dot_t(a, b):
    return lax.dot_general(a, b, (((1,), (b.ndim - 1,)), ((), ())), preferred_element_type=F32)


def core_swap(block):
    count = lax.axis_size("leaf")
    return lax.ppermute(block, "leaf", [(i, i ^ 1) for i in range(count)])


def leaf_groups(size):
    count = lax.axis_size("leaf")
    return [[first + i for i in range(size)] for first in range(0, count, size)]


def leaf_scatter(pieces):
    size = pieces.shape[0]
    return lax.all_to_all(pieces, "leaf", 0, 0, tiled=True, axis_index_groups=leaf_groups(size))


def leaf_everyone(block, size):
    return leaf_scatter(jnp.broadcast_to(block, (size, *block.shape)))


def shards(rhs, inv_diag, off_diag, pair_mask):
    rows_n = lax.axis_size("row")
    leaves = lax.axis_size("leaf")
    levels = leaves.bit_length() - 1
    width = inv_diag.shape[3]
    cols = rhs.shape[3]
    strip = width // rows_n
    half = cols // 2
    sub = half // rows_n
    leaf = lax.axis_index("leaf")
    core = leaf % 2
    first_core = core == 0
    b_all = rhs[0, 0]
    d_all = inv_diag[0, 0]
    panels = off_diag[0, 0]
    live = pair_mask[0, 0]
    heights = [strip >> m for m in range(levels + 1)]
    starts = [sum(heights[:m]) for m in range(levels + 1)]

    def panel(m, l):
        first = column_start(m, l, width)
        return panels[:, first : first + (width >> l)]

    def alive(m, l, dtype):
        return live[m * (m - 1) // 2 + l].astype(dtype)

    def masked(m, l):
        return panel(m, l) * alive(m, l, BF16)

    d_own0 = d_all[: heights[0]]
    d_full0 = lax.all_gather(d_own0, "row", axis=0, tiled=True)
    b0 = b_all[: heights[0]]
    z0 = jnp.concatenate(
        [
            lax.all_gather(b0[:, :half], "row", axis=0, tiled=True),
            lax.all_gather(b0[:, half:], "row", axis=0, tiled=True),
        ],
        axis=1,
    )
    d_own1 = d_all[starts[1] : starts[2]]
    mid = width // 2
    own1 = jnp.concatenate(
        [masked(m, 1) for m in range(2, levels + 1)] + [d_own1[:, :mid], d_own1[:, mid:]], axis=0
    )
    other1 = core_swap(own1)
    p_rows = strip * (levels - 1)
    p_own1 = own1[:p_rows]
    p_other1 = other1[:p_rows]
    d_other1 = jnp.concatenate(
        [other1[p_rows : p_rows + heights[1]], other1[p_rows + heights[1] :]], axis=1
    )
    upper_pairs = sorted(
        ((m, l) for l in range(2, levels) for m in range(l + 1, levels + 1)),
        key=lambda p: (p[1], p[0]),
    )
    d_up = d_all[starts[2] :]
    d_rows = d_up.shape[0]
    d_pad = strip // 2
    d_up = jnp.concatenate([d_up, jnp.zeros((d_pad - d_rows, width), BF16)], axis=0)
    packed = jnp.concatenate(
        [jnp.concatenate([d_up[:, :mid], d_up[:, mid:]], axis=0)]
        + [masked(m, l) for m, l in upper_pairs],
        axis=1,
    )
    packed, d_full0 = lax.optimization_barrier((packed, d_full0))
    everyone = lax.all_gather(packed, "row", axis=0, tiled=False)
    yb0 = dot(d_full0, z0).astype(BF16)
    out0 = dot(d_own0, z0)
    parts = []
    for m in range(1, levels + 1):
        placed = lax.dynamic_update_slice(
            jnp.zeros((strip, cols), BF16),
            b_all[starts[m] : starts[m] + heights[m]],
            (leaf % 2**m * heights[m], 0),
        )
        parts.append(placed.astype(F32) - dot(panel(m, 0), yb0) * alive(m, 0, F32))
    part = jnp.concatenate(parts, axis=0)
    kept = jnp.where(first_core, part[:, :half], part[:, half:])
    sent = jnp.where(first_core, part[:, half:], part[:, :half]).astype(BF16)
    part = kept + core_swap(sent).astype(F32)

    def natural1(block):
        pieces = lax.all_gather(block, "row", axis=0, tiled=False)
        return (
            pieces.reshape(rows_n, 2, heights[1], half).transpose(1, 0, 2, 3).reshape(2, mid, half)
        )

    z1 = natural1(part[:strip].astype(BF16)).reshape(width, half)
    y_own1 = dot(d_own1, z1)
    y_other1 = dot(d_other1, z1)
    yb1 = jnp.where(
        first_core,
        jnp.concatenate([y_own1, y_other1], axis=0),
        jnp.concatenate([y_other1, y_own1], axis=0),
    ).astype(BF16)
    y_got1 = core_swap(y_other1)
    out1 = jnp.where(
        first_core,
        jnp.concatenate([y_own1, y_got1], axis=1),
        jnp.concatenate([y_got1, y_own1], axis=1),
    )
    yn1 = natural1(yb1)
    here = jnp.where(first_core, yn1[0], yn1[1])
    there = jnp.where(first_core, yn1[1], yn1[0])
    part = part[strip:] - (dot(p_own1, here) + dot(p_other1, there))
    turned = part.T.astype(BF16).reshape(rows_n, sub, p_rows)
    turned = lax.all_to_all(turned, "row", 0, 0, tiled=True)

    def turned_of(m):
        return turned[:, :, (m - 2) * strip : (m - 1) * strip]

    def d_leaf(m):
        low = starts[m] - starts[2]
        left = everyone[:, low : low + heights[m], :mid]
        right = everyone[:, d_pad + low : d_pad + low + heights[m], :mid]
        return jnp.concatenate([left, right], axis=2).reshape(rows_n * heights[m], width)

    p_leaf = {}
    at = mid
    for m, l in upper_pairs:
        p_leaf[m, l] = everyone[:, :, at : at + (width >> l)]
        at += width >> l

    def natural(z, m):
        z = z.reshape(rows_n, 2 * sub, 2**m, heights[m])
        return z.transpose(1, 2, 0, 3).reshape(2 * sub, width)

    solved = []
    sums = {}
    for m in range(2, levels + 1):
        if m == 2:
            pieces = leaf_everyone(turned_of(2), 4).astype(F32)
            pieces = pieces.reshape(2, 2, rows_n, sub, strip).sum(axis=0).astype(BF16)
            z = pieces.transpose(1, 0, 2, 3).reshape(rows_n, 2 * sub, strip)
        else:
            size = 2**m
            mine = jnp.where(
                (jnp.arange(2) == core)[None, :, None, None],
                turned_of(m)[:, None],
                jnp.zeros((), BF16),
            ).reshape(rows_n, 2 * sub, strip)
            v = (mine.astype(F32) - sums[m]).astype(BF16)
            if size <= rows_n:
                v = v.reshape(size, rows_n // size, 2 * sub, strip)
                z = leaf_scatter(v).astype(F32).sum(axis=0).astype(BF16)
                z = leaf_everyone(z, size).reshape(rows_n, 2 * sub, strip)
            else:
                cut = size // rows_n
                v = v.reshape(rows_n, 2 * sub, cut, strip // cut).transpose(0, 2, 1, 3)
                v = v.reshape(size, 2 * sub, strip // cut)
                z = leaf_scatter(v).astype(F32).sum(axis=0).astype(BF16)
                z = leaf_everyone(z, size).reshape(rows_n, cut, 2 * sub, strip // cut)
                z = z.transpose(0, 2, 1, 3).reshape(rows_n, 2 * sub, strip)
        y = dot_t(natural(z, m), d_leaf(m))
        yb = y.astype(BF16)
        solved.append(yb.reshape(2 * sub, rows_n, heights[m]))
        for higher in range(m + 1, levels + 1):
            term = dot_t(yb, p_leaf[higher, m]).transpose(1, 0, 2)
            sums[higher] = term if m == 2 else sums[higher] + term
    done = jnp.concatenate(solved, axis=2).transpose(1, 0, 2)
    done = lax.all_to_all(done, "row", 0, 0, tiled=True)
    done = done.reshape(rows_n, 2, sub, d_rows).transpose(3, 1, 0, 2).reshape(d_rows, cols)
    return jnp.concatenate([out0, out1, done.astype(F32)], axis=0)[None, None]


def solution(mesh):
    in_specs = (
        P("leaf", "row", None, None),
        P("leaf", "row", None, None),
        P("leaf", "row", None, None),
        P("leaf", "row", None),
    )
    out_specs = P("leaf", "row", None, None)
    return jax.shard_map(shards, mesh=mesh, in_specs=in_specs, out_specs=out_specs, check_vma=False)
```

profile of v0, /device:TPU:1, one launch (start us, length us, event | category | flops | bytes accessed | tf_op | source)
XLA Modules:
  0.0 420.5 jit_solution(10371558072732546112)
XLA Ops:
  14.2 3.0 slice_multiply_fusion.4
  18.1 67.4 %all-gather.6.cloned.1.call-done = bf16[1,1,1536,1536]{3,2,1,0:T(8,128)(2,1)} async-done(((bf16[1,1,96,1536]{3,2,1,0:T(8,128)(2,1)}), bf16[1,1,1536,1536]{3,2,1,0:T(8,128)(2,1)}) %all-gather.6.cloned.1.call-update) | async-done | bytes 4718608 | tf_op jit(solution)/shard_map/all_gather | solution.py:77
  96.0 10.9 %collective-permute-start.1 = (bf16[480,768]{1,0:T(8,128)(2,1)}, bf16[480,768]{1,0:T(8,128)(2,1)S(1)}, u32[]{:S(2)}, u32[]{:S(2)}) collective-permute-start(bf16[480,768]{1,0:T(8,128)(2,1)} %slice_dynamic-update-slice_fusion), channel_id=1, source_target_pairs={{0,16},{16,0},{32,48},{48,32},{64,80},{80,64},{96,112},{112,96},{1... | collective-permute-start | bytes 2211848 | tf_op jit(solution)/shard_map/ppermute | solution.py:30
  111.7 37.0 %all_gather.25 = bf16[1536,256]{1,0:T(8,128)(2,1)S(1)} all-gather(bf16[96,256]{1,0:T(8,128)(2,1)S(1)} %get-tuple-element.43), channel_id=1, replica_groups=mesh['leaf'=32,'row'=16] {'row'}, dimensions={0}, use_global_device_ids=true | all-gather | bytes 835584 | tf_op jit(solution)/shard_map/all_gather | solution.py:81
  148.8 36.5 %all_gather.26 = bf16[1536,256]{1,0:T(8,128)(2,1)S(1)} all-gather(bf16[96,256]{1,0:T(8,128)(2,1)S(1)} %get-tuple-element.42), channel_id=1, replica_groups=mesh['leaf'=32,'row'=16] {'row'}, dimensions={0}, use_global_device_ids=true | all-gather | bytes 835584 | tf_op jit(solution)/shard_map/all_gather | solution.py:82
  190.1 9.7 %collective-permute-start = (bf16[480,256]{1,0:T(8,128)(2,1)S(1)}, bf16[480,256]{1,0:T(8,128)(2,1)S(1)}, u32[]{:S(2)}, u32[]{:S(2)}) collective-permute-start(bf16[480,256]{1,0:T(8,128)(2,1)S(1)} %select_convert_fusion), channel_id=1, source_target_pairs={{0,16},{16,0},{32,48},{48,32},{64,80},{80,64},{96,112},{112,96},{1... | collective-permute-start | bytes 737288 | tf_op jit(solution)/shard_map/ppermute | solution.py:30
  201.0 25.1 %all-gather.1 = bf16[1536,256]{1,0:T(8,128)(2,1)S(1)} all-gather(bf16[96,256]{1,0:T(8,128)(2,1)S(1)} %slice.485), channel_id=3, replica_groups=mesh['leaf'=32,'row'=16] {'row'}, dimensions={0}, use_global_device_ids=true | all-gather | bytes 835584 | tf_op jit(solution)/shard_map/all_gather | solution.py:129
  228.2 24.3 %all_gather.30 = bf16[16,96,256]{2,1,0:T(8,128)(2,1)S(1)} all-gather(bf16[1,96,256]{2,1,0:T(8,128)(2,1)S(1)} %fusion.61), channel_id=1, replica_groups=mesh['leaf'=32,'row'=16] {'row'}, dimensions={0}, use_global_device_ids=true | all-gather | bytes 835584 | tf_op jit(solution)/shard_map/all_gather | solution.py:129
  253.4 20.8 %all_to_all.45 = bf16[16,16,384]{2,1,0:T(8,128)(2,1)S(1)} all-to-all(bf16[16,16,384]{2,1,0:T(8,128)(2,1)S(1)} %bitcast.226), channel_id=1, replica_groups=mesh['leaf'=32,'row'=16] {'row'}, dimensions={0} | all-to-all | bytes 393216 | tf_op jit(solution)/shard_map/all_to_all | solution.py:153
  275.1 18.8 %all-to-all-start.1 = ((bf16[4,16,16,96]{3,2,1,0:T(8,128)(2,1)}), bf16[4,16,16,96]{3,2,1,0:T(8,128)(2,1)S(1)}, u32[]{:S(2)}, u32[]{:S(2)}) async-start(bf16[4,16,16,96]{3,2,1,0:T(8,128)(2,1)} %broadcast_in_dim.70), calls=%async_computation.1 | async-start | bytes 524288 | tf_op jit(solution)/shard_map/all_to_all | solution.py:40
  312.4 5.2 %all-to-all-start.2 = ((bf16[8,2,32,96]{3,2,1,0:T(8,128)(2,1)}), bf16[8,2,32,96]{3,2,1,0:T(8,128)(2,1)S(1)}, u32[]{:S(2)}, u32[]{:S(2)}) async-start(bf16[8,2,32,96]{3,2,1,0:T(8,128)(2,1)} %bitcast.55), calls=%async_computation.2 | async-start | bytes 262144 | tf_op jit(solution)/shard_map/all_to_all | solution.py:40
  318.7 4.2 all-to-all-done.2
  323.6 4.7 %all-to-all-start.3 = ((bf16[8,2,32,96]{3,2,1,0:T(8,128)(2,1)}), bf16[8,2,32,96]{3,2,1,0:T(8,128)(2,1)}, u32[]{:S(2)}, u32[]{:S(2)}) async-start(bf16[8,2,32,96]{3,2,1,0:T(8,128)(2,1)} %broadcast_in_dim.77), calls=%async_computation.3 | async-start | bytes 262144 | tf_op jit(solution)/shard_map/all_to_all | solution.py:40
  330.5 3.2 all-to-all-done.3
  341.3 4.3 %all-to-all-start.4 = ((bf16[16,1,32,96]{3,2,1,0:T(8,128)(2,1)}), bf16[16,1,32,96]{3,2,1,0:T(8,128)(2,1)S(1)}, u32[]{:S(2)}, u32[]{:S(2)}) async-start(bf16[16,1,32,96]{3,2,1,0:T(8,128)(2,1)} %fusion.36), calls=%async_computation.4 | async-start | bytes 262144 | tf_op jit(solution)/shard_map/all_to_all | solution.py:40
  346.8 4.9 %all-to-all-done.4 = bf16[16,1,32,96]{3,2,1,0:T(8,128)(2,1)S(1)} async-done(((bf16[16,1,32,96]{3,2,1,0:T(8,128)(2,1)}), bf16[16,1,32,96]{3,2,1,0:T(8,128)(2,1)S(1)}, u32[]{:S(2)}, u32[]{:S(2)}) %all-to-all-start.4) | async-done | bytes 98336 | tf_op jit(solution)/shard_map/all_to_all | solution.py:40
  352.4 4.0 all-to-all-start.5
  358.8 3.8 all-to-all-done.5
  366.2 5.6 %all-to-all-start.6 = ((bf16[32,2,768]{2,1,0:T(2,128)(2,1)}), bf16[32,2,768]{2,1,0:T(2,128)(2,1)S(1)}, u32[]{:S(2)}, u32[]{:S(2)}) async-start(bf16[32,2,768]{2,1,0:T(2,128)(2,1)} %reshape.243), calls=%async_computation.6 | async-start | bytes 196608 | tf_op jit(solution)/shard_map/all_to_all | solution.py:40
  373.0 6.3 %all-to-all-done.6 = bf16[32,2,768]{2,1,0:T(2,128)(2,1)S(1)} async-done(((bf16[32,2,768]{2,1,0:T(2,128)(2,1)}), bf16[32,2,768]{2,1,0:T(2,128)(2,1)S(1)}, u32[]{:S(2)}, u32[]{:S(2)}) %all-to-all-start.6) | async-done | bytes 98336 | tf_op jit(solution)/shard_map/all_to_all | solution.py:40
  380.7 3.9 all-to-all-start.7
  386.0 6.1 %all-to-all-done.7 = bf16[32,2,768]{2,1,0:T(2,128)(2,1)S(1)} async-done(((bf16[32,2,768]{2,1,0:T(2,128)(2,1)}), bf16[32,2,768]{2,1,0:T(2,128)(2,1)S(1)}, u32[]{:S(2)}, u32[]{:S(2)}) %all-to-all-start.7) | async-done | bytes 98336 | tf_op jit(solution)/shard_map/all_to_all | solution.py:40
  395.8 4.8 %all-to-all-start.8 = ((bf16[16,2,720]{2,1,0:T(2,128)(2,1)}), bf16[16,2,720]{2,1,0:T(2,128)(2,1)S(1)}, u32[]{:S(2)}, u32[]{:S(2)}) async-start(bf16[16,2,720]{2,1,0:T(2,128)(2,1)} %reshape.247), calls=%async_computation.8 | async-start | bytes 98304 | tf_op jit(solution)/shard_map/all_to_all | solution.py:207
  401.9 10.3 %all-to-all-done.8 = bf16[16,2,720]{2,1,0:T(2,128)(2,1)S(1)} async-done(((bf16[16,2,720]{2,1,0:T(2,128)(2,1)}), bf16[16,2,720]{2,1,0:T(2,128)(2,1)S(1)}, u32[]{:S(2)}, u32[]{:S(2)}) %all-to-all-start.8) | async-done | bytes 46112 | tf_op jit(solution)/shard_map/all_to_all | solution.py:207
  (160 shorter events, 78.3 us)
Async XLA Ops:
  6.5 78.9 %all-gather.6.cloned.1.call-start = ((), (), s32[]{:S(2)}) async-start(), calls=%async_computation.9 | async-start | bytes 5013504 | tf_op jit(solution)/shard_map/all_gather | solution.py:77
  8.3 292.4 %all-gather.8.cloned.1.call-start = ((), (), s32[]{:S(2)}) async-start(), calls=%async_computation.10 | async-start | bytes 7938048 | tf_op jit(solution)/shard_map/all_gather | solution.py:112
  17.2 77.5 %copy-start.1 = (bf16[1,1,189,1536]{3,2,1,0:T(8,128)(2,1)S(1)}, bf16[1,1,189,1536]{3,2,1,0:T(8,128)(2,1)}, u32[]{:S(2)}) copy-start(bf16[1,1,189,1536]{3,2,1,0:T(8,128)(2,1)} %param.5) | copy-start | bytes 1741828
  18.1 88.8 %copy-start.13 = (s32[1,1,15]{2,1,0:T(1,128)S(1)}, s32[1,1,15]{2,1,0:T(1,128)}, u32[]{:S(2)}) copy-start(s32[1,1,15]{2,1,0:T(1,128)} %param.7) | copy-start | bytes 184
  18.1 92.8 %copy-start.9 = (bf16[1,1,189,512]{3,2,1,0:T(8,128)(2,1)S(1)}, bf16[1,1,189,512]{3,2,1,0:T(8,128)(2,1)}, u32[]{:S(2)}) copy-start(bf16[1,1,189,512]{3,2,1,0:T(8,128)(2,1)} %param.4) | copy-start | bytes 580612
  96.0 103.9 %collective-permute-start.1 = (bf16[480,768]{1,0:T(8,128)(2,1)}, bf16[480,768]{1,0:T(8,128)(2,1)S(1)}, u32[]{:S(2)}, u32[]{:S(2)}) collective-permute-start(bf16[480,768]{1,0:T(8,128)(2,1)} %slice_dynamic-update-slice_fusion), channel_id=1, source_target_pairs={{0,16},{16,0},{32,48},{48,32},{64,80},{80,64},{96,112},{112,96},{1... | collective-permute-start | bytes 2211848 | tf_op jit(solution)/shard_map/ppermute | solution.py:30
  111.7 73.6 %copy-start.14 = (bf16[1,1,1536,1536]{3,2,1,0:T(8,128)(2,1)S(1)}, bf16[1,1,1536,1536]{3,2,1,0:T(8,128)(2,1)}, u32[]{:S(2)}) copy-start(bf16[1,1,1536,1536]{3,2,1,0:T(8,128)(2,1)} %all-gather.6.cloned.1.call-done) | copy-start | bytes 14155780
  190.1 10.9 %collective-permute-start = (bf16[480,256]{1,0:T(8,128)(2,1)S(1)}, bf16[480,256]{1,0:T(8,128)(2,1)S(1)}, u32[]{:S(2)}, u32[]{:S(2)}) collective-permute-start(bf16[480,256]{1,0:T(8,128)(2,1)S(1)} %select_convert_fusion), channel_id=1, source_target_pairs={{0,16},{16,0},{32,48},{48,32},{64,80},{80,64},{96,112},{112,96},{1... | collective-permute-start | bytes 737288 | tf_op jit(solution)/shard_map/ppermute | solution.py:30
  227.1 25.5 %copy-start.10 = (bf16[96,768]{1,0:T(8,128)(2,1)S(1)}, bf16[96,768]{1,0:T(8,128)(2,1)}, u32[]{:S(2)}) copy-start(bf16[96,768]{1,0:T(8,128)(2,1)} %get-tuple-element.14) | copy-start | bytes 442372
  227.1 25.5 %copy-start.11 = (bf16[96,768]{1,0:T(8,128)(2,1)S(1)}, bf16[96,768]{1,0:T(8,128)(2,1)}, u32[]{:S(2)}) copy-start(bf16[96,768]{1,0:T(8,128)(2,1)} %get-tuple-element.12) | copy-start | bytes 442372
  227.1 25.5 %copy-start.12 = (bf16[96,768]{1,0:T(8,128)(2,1)S(1)}, bf16[96,768]{1,0:T(8,128)(2,1)}, u32[]{:S(2)}) copy-start(bf16[96,768]{1,0:T(8,128)(2,1)} %get-tuple-element.10) | copy-start | bytes 442372
  227.3 25.6 %copy-start.7 = (f32[256,48]{0,1:T(8,128)}, f32[256,48]{0,1:T(8,128)S(1)}, u32[]{:S(2)}) copy-start(f32[256,48]{0,1:T(8,128)S(1)} %fusion.70) | copy-start | bytes 147460
  275.1 23.9 %all-to-all-start.1 = ((bf16[4,16,16,96]{3,2,1,0:T(8,128)(2,1)}), bf16[4,16,16,96]{3,2,1,0:T(8,128)(2,1)S(1)}, u32[]{:S(2)}, u32[]{:S(2)}) async-start(bf16[4,16,16,96]{3,2,1,0:T(8,128)(2,1)} %broadcast_in_dim.70), calls=%async_computation.1 | async-start | bytes 524288 | tf_op jit(solution)/shard_map/all_to_all | solution.py:40
  294.1 106.8 %collective-permute-start.2 = (f32[48,256]{1,0:T(8,128)}, f32[48,256]{1,0:T(8,128)}, u32[]{:S(2)}, u32[]{:S(2)}) collective-permute-start(f32[48,256]{1,0:T(8,128)} %fusion.57), channel_id=1, source_target_pairs={{0,16},{16,0},{32,48},{48,32},{64,80},{80,64},{96,112},{112,96},{1... | collective-permute-start | bytes 147464 | tf_op jit(solution)/shard_map/ppermute | solution.py:30
  312.4 10.5 %all-to-all-start.2 = ((bf16[8,2,32,96]{3,2,1,0:T(8,128)(2,1)}), bf16[8,2,32,96]{3,2,1,0:T(8,128)(2,1)S(1)}, u32[]{:S(2)}, u32[]{:S(2)}) async-start(bf16[8,2,32,96]{3,2,1,0:T(8,128)(2,1)} %bitcast.55), calls=%async_computation.2 | async-start | bytes 262144 | tf_op jit(solution)/shard_map/all_to_all | solution.py:40
  323.6 10.1 %all-to-all-start.3 = ((bf16[8,2,32,96]{3,2,1,0:T(8,128)(2,1)}), bf16[8,2,32,96]{3,2,1,0:T(8,128)(2,1)}, u32[]{:S(2)}, u32[]{:S(2)}) async-start(bf16[8,2,32,96]{3,2,1,0:T(8,128)(2,1)} %broadcast_in_dim.77), calls=%async_computation.3 | async-start | bytes 262144 | tf_op jit(solution)/shard_map/all_to_all | solution.py:40
  330.5 8.5 %copy-start.6 = (bf16[16,32,96]{2,1,0:T(8,128)(2,1)S(1)}, bf16[16,32,96]{2,1,0:T(8,128)(2,1)}, u32[]{:S(2)}) copy-start(bf16[16,32,96]{2,1,0:T(8,128)(2,1)} %get-tuple-element.44) | copy-start | bytes 294916
  339.0 17.4 %copy-start.2 = (f32[32,16,96]{2,0,1:T(8,128)S(1)}, f32[32,16,96]{2,0,1:T(8,128)}, u32[]{:S(2)}) copy-start(f32[32,16,96]{2,0,1:T(8,128)} %fusion) | copy-start | bytes 589828
  341.3 10.4 %all-to-all-start.4 = ((bf16[16,1,32,96]{3,2,1,0:T(8,128)(2,1)}), bf16[16,1,32,96]{3,2,1,0:T(8,128)(2,1)S(1)}, u32[]{:S(2)}, u32[]{:S(2)}) async-start(bf16[16,1,32,96]{3,2,1,0:T(8,128)(2,1)} %fusion.36), calls=%async_computation.4 | async-start | bytes 262144 | tf_op jit(solution)/shard_map/all_to_all | solution.py:40
  352.4 10.2 %all-to-all-start.5 = ((bf16[16,1,32,96]{3,2,1,0:T(8,128)(2,1)}), bf16[16,1,32,96]{3,2,1,0:T(8,128)(2,1)S(1)}, u32[]{:S(2)}, u32[]{:S(2)}) async-start(bf16[16,1,32,96]{3,2,1,0:T(8,128)(2,1)} %broadcast_in_dim.80), calls=%async_computation.5 | async-start | bytes 262144 | tf_op jit(solution)/shard_map/all_to_all | solution.py:40
  365.2 19.5 %copy-start.4 = (bf16[32,384]{1,0:T(8,128)(2,1)S(1)}, bf16[32,384]{1,0:T(8,128)(2,1)}, u32[]{:S(2)}) copy-start(bf16[32,384]{1,0:T(8,128)(2,1)} %copy-done.3) | copy-start | bytes 73732
  366.2 13.1 %all-to-all-start.6 = ((bf16[32,2,768]{2,1,0:T(2,128)(2,1)}), bf16[32,2,768]{2,1,0:T(2,128)(2,1)S(1)}, u32[]{:S(2)}, u32[]{:S(2)}) async-start(bf16[32,2,768]{2,1,0:T(2,128)(2,1)} %reshape.243), calls=%async_computation.6 | async-start | bytes 196608 | tf_op jit(solution)/shard_map/all_to_all | solution.py:40
  380.7 11.5 %all-to-all-start.7 = ((bf16[32,2,768]{2,1,0:T(2,128)(2,1)}), bf16[32,2,768]{2,1,0:T(2,128)(2,1)S(1)}, u32[]{:S(2)}, u32[]{:S(2)}) async-start(bf16[32,2,768]{2,1,0:T(2,128)(2,1)} %reshape.245), calls=%async_computation.7 | async-start | bytes 196608 | tf_op jit(solution)/shard_map/all_to_all | solution.py:40
  395.8 16.4 %all-to-all-start.8 = ((bf16[16,2,720]{2,1,0:T(2,128)(2,1)}), bf16[16,2,720]{2,1,0:T(2,128)(2,1)S(1)}, u32[]{:S(2)}, u32[]{:S(2)}) async-start(bf16[16,2,720]{2,1,0:T(2,128)(2,1)} %reshape.247), calls=%async_computation.8 | async-start | bytes 98304 | tf_op jit(solution)/shard_map/all_to_all | solution.py:207
  (4 other events, 22.4 us)
Sparse Core Ops, SparseCore 0:
  9.4 76.0 all-gather.5
  87.5 117.3 all-gather.7
where the time goes:
time: 422 us; the launch traced here: 421 us
  blocking collectives  144 us (34%)
  waiting for transfers between devices  109 us (26%)
  starting transfers between devices  73.9 us (18%)
  local copies, waits for them, and re-layouts  30 us (7%)
  matrix products  23.1 us (5%)
  other arithmetic  23 us (5%)
  between operations  17.6 us (4%)
    all_gather x1, waiting for transfers between devices, shards(): d_full0 = lax.all_gather(d_own0, 'row', axis=0, tiled=True)  67.4 us
    all_gather x2, blocking collectives, natural1(): pieces = lax.all_gather(block, 'row', axis=0, tiled=False)  49.4 us
    all_to_all x7, starting transfers between devices, leaf_scatter(): lax.all_to_all(pieces, 'leaf', 0, 0, tiled=True, axis_index_groups=leaf_g...  46.5 us
    all_gather x1, blocking collectives, shards(): lax.all_gather(b0[:, :half], 'row', axis=0, tiled=True)  37 us
    all_gather x1, blocking collectives, shards(): lax.all_gather(b0[:, half:], 'row', axis=0, tiled=True)  36.5 us
    all_to_all x7, waiting for transfers between devices, leaf_scatter(): lax.all_to_all(pieces, 'leaf', 0, 0, tiled=True, axis_index_groups=leaf_g...  30.6 us
    ppermute x3, starting transfers between devices, core_swap(): return lax.ppermute(block, 'leaf', [(i, i ^ 1) for i in range(count)])  22.5 us
    all_to_all x1, blocking collectives, shards(): turned = lax.all_to_all(turned, 'row', 0, 0, tiled=True)  20.8 us
  transfers between devices with their start and end apart: 13, of which 10 were waited for; matrix products, arithmetic and copies ran while one was open for 17% of the time, Pallas kernels for 0%

commit v1 on v0

--- a/solution.py
+++ b/solution.py
@@ -5,6 +5,28 @@
 
 F32 = jnp.float32
 BF16 = jnp.bfloat16
+
+
+def joined_along(blocks, dim):
+    shape = list(blocks.shape[1:])
+    shape[dim] *= blocks.shape[0]
+    return jnp.moveaxis(blocks, 0, dim).reshape(shape)
+
+
+def ring_gather(x, axis, dim):
+    devices = lax.axis_size(axis)
+    pairs = [(i, (i + 1) % devices) for i in range(devices)]
+    back = [(b, a) for a, b in pairs]
+    lower, upper = ([], [])
+    for turn in range(devices - 1):
+        if turn % 2 == 0:
+            lower.append(lax.ppermute(lower[-1] if lower else x, axis, pairs))
+        else:
+            upper.append(lax.ppermute(upper[-1] if upper else x, axis, back))
+    parts = jnp.stack([*lower[::-1], x, *upper])
+    shift = lax.axis_index(axis) - len(lower)
+    parts = parts[(jnp.arange(devices) - shift) % devices]
+    return joined_along(parts, dim)
 
 
 def column_start(ancestor, source, width_all):
@@ -79,7 +101,7 @@
     z0 = jnp.concatenate(
         [
             lax.all_gather(b0[:, :half], "row", axis=0, tiled=True),
-            lax.all_gather(b0[:, half:], "row", axis=0, tiled=True),
+            ring_gather(b0[:, half:], "row", 0),
         ],
         axis=1,
     )

time: 422 us -> 462 us (1.095)
  starting transfers between devices: 73.9 us -> 124 us
  blocking collectives: 144 us -> 107 us
  local copies, waits for them, and re-layouts: 30 us -> 52.8 us
  waiting for transfers between devices: 109 us -> 116 us
  other arithmetic: 23 us -> 16.6 us
    ppermute x0 -> x15, starting transfers between devices: none -> 49.2 us  [the longest x7 31.3 us: ring_gather(): upper.append(lax.ppermute(upper[-1] if upper else x, axis, back))]
    all_gather x1 -> x0, blocking collectives: 36.5 us -> none  [shards(): lax.all_gather(b0[:, half:], 'row', axis=0, tiled=True)]
    unnamed x38 -> x54, local copies, waits for them, and re-layouts: 4.29 us -> 23.9 us
    ppermute x0 -> x15, waiting for transfers between devices: none -> 6.89 us  [the longest x8 6.87 us: ring_gather(): lower.append(lax.ppermute(lower[-1] if lower else x, axis, pairs))]
  transfers between devices with their start and end apart: 13 -> 28, of which waited for: 10 -> 16; matrix products, arithmetic and copies ran while one was open for 17% -> 20% of each run, Pallas kernels for 0% -> 0%
where the time goes in v1:
time: 462 us; the launch traced here: 459 us
  starting transfers between devices  124 us (27%)
  waiting for transfers between devices  116 us (25%)
  blocking collectives  107 us (23%)
  local copies, waits for them, and re-layouts  52.8 us (11%)
  matrix products  24.2 us (5%)
  between operations  17.6 us (4%)
  other arithmetic  16.6 us (4%)
    all_gather x1, waiting for transfers between devices, shards(): d_full0 = lax.all_gather(d_own0, 'row', axis=0, tiled=True)  65.2 us
    all_gather x2, blocking collectives, natural1(): pieces = lax.all_gather(block, 'row', axis=0, tiled=False)  50.6 us
    all_to_all x7, starting transfers between devices, leaf_scatter(): lax.all_to_all(pieces, 'leaf', 0, 0, tiled=True, axis_index_groups=leaf_g...  46.1 us
    all_gather x1, blocking collectives, shards(): lax.all_gather(b0[:, :half], 'row', axis=0, tiled=True)  37.4 us
    all_to_all x7, waiting for transfers between devices, leaf_scatter(): lax.all_to_all(pieces, 'leaf', 0, 0, tiled=True, axis_index_groups=leaf_g...  34.7 us
    ppermute x7, starting transfers between devices, ring_gather(): upper.append(lax.ppermute(upper[-1] if upper else x, axis, back))  31.3 us
    ppermute x3, starting transfers between devices, core_swap(): return lax.ppermute(block, 'leaf', [(i, i ^ 1) for i in range(count)])  24.1 us
    unnamed x54, local copies, waits for them, and re-layouts  23.9 us
  transfers between devices with their start and end apart: 28, of which 16 were waited for; matrix products, arithmetic and copies ran while one was open for 20% of the time, Pallas kernels for 0%

profile of v1, /device:TPU:1, one launch (start us, length us, event | category | flops | bytes accessed | tf_op | source)
XLA Modules:
  0.0 458.8 jit_solution(8008954051516240355)
XLA Ops:
  20.2 65.2 %all-gather.6.cloned.1.call-done = bf16[1,1,1536,1536]{3,2,1,0:T(8,128)(2,1)} async-done(((bf16[1,1,96,1536]{3,2,1,0:T(8,128)(2,1)}), bf16[1,1,1536,1536]{3,2,1,0:T(8,128)(2,1)}) %all-gather.6.cloned.1.call-update) | async-done | bytes 4718608 | tf_op jit(solution)/shard_map/all_gather | solution.py:99
  98.9 11.4 %collective-permute-start.16 = (bf16[480,768]{1,0:T(8,128)(2,1)}, bf16[480,768]{1,0:T(8,128)(2,1)}, u32[]{:S(2)}, u32[]{:S(2)}) collective-permute-start(bf16[480,768]{1,0:T(8,128)(2,1)} %slice_dynamic-update-slice_fusion), channel_id=1, source_target_pairs={{0,16},{16,0},{32,48},{48,32},{64,80},{80,64},{96,112},{112,96},{1... | collective-permute-start | bytes 2211848 | tf_op jit(solution)/shard_map/ppermute | solution.py:52
  110.3 37.4 %all_gather.22 = bf16[1536,256]{1,0:T(8,128)(2,1)} all-gather(bf16[96,256]{1,0:T(8,128)(2,1)S(1)} %get-tuple-element.42), channel_id=1, replica_groups=mesh['leaf'=32,'row'=16] {'row'}, dimensions={0}, use_global_device_ids=true | all-gather | bytes 835584 | tf_op jit(solution)/shard_map/all_gather | solution.py:103
  159.1 4.2 collective-permute-start.9
  166.4 4.6 collective-permute-start.10
  174.0 4.6 collective-permute-start.11
  181.6 4.6 collective-permute-start.12
  189.0 4.9 %collective-permute-start.13 = (bf16[96,256]{1,0:T(8,128)(2,1)}, bf16[96,256]{1,0:T(8,128)(2,1)}, u32[]{:S(2)}, u32[]{:S(2)}) collective-permute-start(bf16[96,256]{1,0:T(8,128)(2,1)} %collective-permute-done.12), channel_id=1, source_target_pairs={{1,0},{2,1},{3,2},{4,3},{5,4},{6,5},{7,6},{8,7},{9,8},{10,9},{11,1... | collective-permute-start | bytes 147464 | tf_op jit(solution)/shard_map/ppermute | solution.py:25
  201.3 4.6 collective-permute-start.14
  228.8 5.4 %convolution_convert_fusion = bf16[1536,512]{1,0:T(8,128)(2,1)S(1)} fusion(bf16[1536,1536]{1,0:T(8,128)(2,1)} %bitcast.268, bf16[1536,256]{1,0:T(8,128)(2,1)} %bitcast.259, bf16[1536,256]{1,0:T(8,128)(2,1)} %all_gather.22), kind=kOutput, calls=%fused_computation.1 | convolution fusion | flops 2419851264 | bytes 7864320 | tf_op jit(solution)/shard_map/dot_general | solution.py:43
  236.4 10.7 %collective-permute-start.15 = (bf16[480,256]{1,0:T(8,128)(2,1)S(1)}, bf16[480,256]{1,0:T(8,128)(2,1)S(1)}, u32[]{:S(2)}, u32[]{:S(2)}) collective-permute-start(bf16[480,256]{1,0:T(8,128)(2,1)S(1)} %select_convert_fusion), channel_id=1, source_target_pairs={{0,16},{16,0},{32,48},{48,32},{64,80},{80,64},{96,112},{112,96},{1... | collective-permute-start | bytes 737288 | tf_op jit(solution)/shard_map/ppermute | solution.py:52
  248.3 24.3 %all-gather.1 = bf16[1536,256]{1,0:T(8,128)(2,1)S(1)} all-gather(bf16[96,256]{1,0:T(8,128)(2,1)S(1)} %slice.488), channel_id=3, replica_groups=mesh['leaf'=32,'row'=16] {'row'}, dimensions={0}, use_global_device_ids=true | all-gather | bytes 835584 | tf_op jit(solution)/shard_map/all_gather | solution.py:151
  273.3 26.2 %all_gather.26 = bf16[16,96,256]{2,1,0:T(8,128)(2,1)S(1)} all-gather(bf16[1,96,256]{2,1,0:T(8,128)(2,1)S(1)} %fusion.61), channel_id=1, replica_groups=mesh['leaf'=32,'row'=16] {'row'}, dimensions={0}, use_global_device_ids=true | all-gather | bytes 835584 | tf_op jit(solution)/shard_map/all_gather | solution.py:151
  301.5 19.0 %all_to_all.45 = bf16[16,16,384]{2,1,0:T(8,128)(2,1)S(1)} all-to-all(bf16[16,16,384]{2,1,0:T(8,128)(2,1)S(1)} %bitcast.261), channel_id=1, replica_groups=mesh['leaf'=32,'row'=16] {'row'}, dimensions={0} | all-to-all | bytes 393216 | tf_op jit(solution)/shard_map/all_to_all | solution.py:175
  321.4 19.1 %all-to-all-start.1 = ((bf16[4,16,16,96]{3,2,1,0:T(8,128)(2,1)}), bf16[4,16,16,96]{3,2,1,0:T(8,128)(2,1)S(1)}, u32[]{:S(2)}, u32[]{:S(2)}) async-start(bf16[4,16,16,96]{3,2,1,0:T(8,128)(2,1)} %broadcast_in_dim.71), calls=%async_computation.1 | async-start | bytes 524288 | tf_op jit(solution)/shard_map/all_to_all | solution.py:62
  356.8 5.3 %all-to-all-start.2 = ((bf16[8,2,32,96]{3,2,1,0:T(8,128)(2,1)}), bf16[8,2,32,96]{3,2,1,0:T(8,128)(2,1)S(1)}, u32[]{:S(2)}, u32[]{:S(2)}) async-start(bf16[8,2,32,96]{3,2,1,0:T(8,128)(2,1)} %bitcast.73), calls=%async_computation.2 | async-start | bytes 262144 | tf_op jit(solution)/shard_map/all_to_all | solution.py:62
  362.2 5.2 %all-to-all-done.2 = bf16[8,2,32,96]{3,2,1,0:T(8,128)(2,1)S(1)} async-done(((bf16[8,2,32,96]{3,2,1,0:T(8,128)(2,1)}), bf16[8,2,32,96]{3,2,1,0:T(8,128)(2,1)S(1)}, u32[]{:S(2)}, u32[]{:S(2)}) %all-to-all-start.2) | async-done | bytes 98336 | tf_op jit(solution)/shard_map/all_to_all | solution.py:62
  385.1 6.0 %all-to-all-done.4 = bf16[16,1,32,96]{3,2,1,0:T(8,128)(2,1)S(1)} async-done(((bf16[16,1,32,96]{3,2,1,0:T(8,128)(2,1)}), bf16[16,1,32,96]{3,2,1,0:T(8,128)(2,1)S(1)}, u32[]{:S(2)}, u32[]{:S(2)}) %all-to-all-start.4) | async-done | bytes 98336 | tf_op jit(solution)/shard_map/all_to_all | solution.py:62
  397.4 4.5 all-to-all-done.5
  405.5 5.5 %all-to-all-start.6 = ((bf16[32,2,768]{2,1,0:T(2,128)(2,1)}), bf16[32,2,768]{2,1,0:T(2,128)(2,1)S(1)}, u32[]{:S(2)}, u32[]{:S(2)}) async-start(bf16[32,2,768]{2,1,0:T(2,128)(2,1)} %reshape.304), calls=%async_computation.6 | async-start | bytes 196608 | tf_op jit(solution)/shard_map/all_to_all | solution.py:62
  412.1 6.3 %all-to-all-done.6 = bf16[32,2,768]{2,1,0:T(2,128)(2,1)S(1)} async-done(((bf16[32,2,768]{2,1,0:T(2,128)(2,1)}), bf16[32,2,768]{2,1,0:T(2,128)(2,1)S(1)}, u32[]{:S(2)}, u32[]{:S(2)}) %all-to-all-start.6) | async-done | bytes 98336 | tf_op jit(solution)/shard_map/all_to_all | solution.py:62
  424.6 6.8 %all-to-all-done.7 = bf16[32,2,768]{2,1,0:T(2,128)(2,1)S(1)} async-done(((bf16[32,2,768]{2,1,0:T(2,128)(2,1)}), bf16[32,2,768]{2,1,0:T(2,128)(2,1)S(1)}, u32[]{:S(2)}, u32[]{:S(2)}) %all-to-all-start.7) | async-done | bytes 98336 | tf_op jit(solution)/shard_map/all_to_all | solution.py:62
  434.0 4.8 %all-to-all-start.8 = ((bf16[16,2,720]{2,1,0:T(2,128)(2,1)}), bf16[16,2,720]{2,1,0:T(2,128)(2,1)S(1)}, u32[]{:S(2)}, u32[]{:S(2)}) async-start(bf16[16,2,720]{2,1,0:T(2,128)(2,1)} %reshape.308), calls=%async_computation.8 | async-start | bytes 98304 | tf_op jit(solution)/shard_map/all_to_all | solution.py:229
  441.2 9.1 %all-to-all-done.8 = bf16[16,2,720]{2,1,0:T(2,128)(2,1)S(1)} async-done(((bf16[16,2,720]{2,1,0:T(2,128)(2,1)}), bf16[16,2,720]{2,1,0:T(2,128)(2,1)S(1)}, u32[]{:S(2)}, u32[]{:S(2)}) %all-to-all-start.8) | async-done | bytes 46112 | tf_op jit(solution)/shard_map/all_to_all | solution.py:229
  (208 shorter events, 141.4 us)
Async XLA Ops:
  6.5 78.9 %all-gather.6.cloned.1.call-start = ((), (), s32[]{:S(2)}) async-start(), calls=%async_computation.9 | async-start | bytes 5013504 | tf_op jit(solution)/shard_map/all_gather | solution.py:99
  8.4 338.8 %all-gather.8.cloned.1.call-start = ((), (), s32[]{:S(2)}) async-start(), calls=%async_computation.10 | async-start | bytes 7938048 | tf_op jit(solution)/shard_map/all_gather | solution.py:134
  85.5 63.0 %collective-permute-start = (bf16[96,256]{1,0:T(8,128)(2,1)S(1)}, bf16[96,256]{1,0:T(8,128)(2,1)S(1)}, u32[]{:S(2)}, u32[]{:S(2)}) collective-permute-start(bf16[96,256]{1,0:T(8,128)(2,1)S(1)} %get-tuple-element.43), channel_id=1, source_target_pairs={{0,1},{1,2},{2,3},{3,4},{4,5},{5,6},{6,7},{7,8},{8,9},{9,10},{10,1... | collective-permute-start | bytes 147464 | tf_op jit(solution)/shard_map/ppermute | solution.py:23
  88.2 70.9 %collective-permute-start.8 = (bf16[96,256]{1,0:T(8,128)(2,1)S(1)}, bf16[96,256]{1,0:T(8,128)(2,1)S(1)}, u32[]{:S(2)}, u32[]{:S(2)}) collective-permute-start(bf16[96,256]{1,0:T(8,128)(2,1)S(1)} %get-tuple-element.43), channel_id=1, source_target_pairs={{1,0},{2,1},{3,2},{4,3},{5,4},{6,5},{7,6},{8,7},{9,8},{10,9},{11,1... | collective-permute-start | bytes 147464 | tf_op jit(solution)/shard_map/ppermute | solution.py:25
  98.9 148.2 %collective-permute-start.16 = (bf16[480,768]{1,0:T(8,128)(2,1)}, bf16[480,768]{1,0:T(8,128)(2,1)}, u32[]{:S(2)}, u32[]{:S(2)}) collective-permute-start(bf16[480,768]{1,0:T(8,128)(2,1)} %slice_dynamic-update-slice_fusion), channel_id=1, source_target_pairs={{0,16},{16,0},{32,48},{48,32},{64,80},{80,64},{96,112},{112,96},{1... | collective-permute-start | bytes 2211848 | tf_op jit(solution)/shard_map/ppermute | solution.py:52
  148.6 7.6 %collective-permute-start.1 = (bf16[96,256]{1,0:T(8,128)(2,1)S(1)}, bf16[96,256]{1,0:T(8,128)(2,1)S(1)}, u32[]{:S(2)}, u32[]{:S(2)}) collective-permute-start(bf16[96,256]{1,0:T(8,128)(2,1)S(1)} %collective-permute-done), channel_id=1, source_target_pairs={{0,1},{1,2},{2,3},{3,4},{4,5},{5,6},{6,7},{7,8},{8,9},{9,10},{10,1... | collective-permute-start | bytes 147464 | tf_op jit(solution)/shard_map/ppermute | solution.py:23
  156.2 7.6 %collective-permute-start.2 = (bf16[96,256]{1,0:T(8,128)(2,1)S(1)}, bf16[96,256]{1,0:T(8,128)(2,1)S(1)}, u32[]{:S(2)}, u32[]{:S(2)}) collective-permute-start(bf16[96,256]{1,0:T(8,128)(2,1)S(1)} %collective-permute-done.1), channel_id=1, source_target_pairs={{0,1},{1,2},{2,3},{3,4},{4,5},{5,6},{6,7},{7,8},{8,9},{9,10},{10,1... | collective-permute-start | bytes 147464 | tf_op jit(solution)/shard_map/ppermute | solution.py:23
  163.8 7.6 %collective-permute-start.3 = (bf16[96,256]{1,0:T(8,128)(2,1)S(1)}, bf16[96,256]{1,0:T(8,128)(2,1)S(1)}, u32[]{:S(2)}, u32[]{:S(2)}) collective-permute-start(bf16[96,256]{1,0:T(8,128)(2,1)S(1)} %collective-permute-done.2), channel_id=1, source_target_pairs={{0,1},{1,2},{2,3},{3,4},{4,5},{5,6},{6,7},{7,8},{8,9},{9,10},{10,1... | collective-permute-start | bytes 147464 | tf_op jit(solution)/shard_map/ppermute | solution.py:23
  171.4 7.6 %collective-permute-start.4 = (bf16[96,256]{1,0:T(8,128)(2,1)S(1)}, bf16[96,256]{1,0:T(8,128)(2,1)}, u32[]{:S(2)}, u32[]{:S(2)}) collective-permute-start(bf16[96,256]{1,0:T(8,128)(2,1)S(1)} %collective-permute-done.3), channel_id=1, source_target_pairs={{0,1},{1,2},{2,3},{3,4},{4,5},{5,6},{6,7},{7,8},{8,9},{9,10},{10,1... | collective-permute-start | bytes 147464 | tf_op jit(solution)/shard_map/ppermute | solution.py:23
  179.0 8.1 %collective-permute-start.5 = (bf16[96,256]{1,0:T(8,128)(2,1)}, bf16[96,256]{1,0:T(8,128)(2,1)}, u32[]{:S(2)}, u32[]{:S(2)}) collective-permute-start(bf16[96,256]{1,0:T(8,128)(2,1)} %collective-permute-done.4), channel_id=1, source_target_pairs={{0,1},{1,2},{2,3},{3,4},{4,5},{5,6},{6,7},{7,8},{8,9},{9,10},{10,1... | collective-permute-start | bytes 147464 | tf_op jit(solution)/shard_map/ppermute | solution.py:23
  187.1 8.3 %collective-permute-start.6 = (bf16[96,256]{1,0:T(8,128)(2,1)}, bf16[96,256]{1,0:T(8,128)(2,1)}, u32[]{:S(2)}, u32[]{:S(2)}) collective-permute-start(bf16[96,256]{1,0:T(8,128)(2,1)} %collective-permute-done.5), channel_id=1, source_target_pairs={{0,1},{1,2},{2,3},{3,4},{4,5},{5,6},{6,7},{7,8},{8,9},{9,10},{10,1... | collective-permute-start | bytes 147464 | tf_op jit(solution)/shard_map/ppermute | solution.py:23
  189.0 12.3 %collective-permute-start.13 = (bf16[96,256]{1,0:T(8,128)(2,1)}, bf16[96,256]{1,0:T(8,128)(2,1)}, u32[]{:S(2)}, u32[]{:S(2)}) collective-permute-start(bf16[96,256]{1,0:T(8,128)(2,1)} %collective-permute-done.12), channel_id=1, source_target_pairs={{1,0},{2,1},{3,2},{4,3},{5,4},{6,5},{7,6},{8,7},{9,8},{10,9},{11,1... | collective-permute-start | bytes 147464 | tf_op jit(solution)/shard_map/ppermute | solution.py:25
  195.4 10.5 %collective-permute-start.7 = (bf16[96,256]{1,0:T(8,128)(2,1)}, bf16[96,256]{1,0:T(8,128)(2,1)}, u32[]{:S(2)}, u32[]{:S(2)}) collective-permute-start(bf16[96,256]{1,0:T(8,128)(2,1)} %collective-permute-done.6), channel_id=1, source_target_pairs={{0,1},{1,2},{2,3},{3,4},{4,5},{5,6},{6,7},{7,8},{8,9},{9,10},{10,1... | collective-permute-start | bytes 147464 | tf_op jit(solution)/shard_map/ppermute | solution.py:23
  201.3 24.3 %collective-permute-start.14 = (bf16[96,256]{1,0:T(8,128)(2,1)}, bf16[96,256]{1,0:T(8,128)(2,1)S(1)}, u32[]{:S(2)}, u32[]{:S(2)}) collective-permute-start(bf16[96,256]{1,0:T(8,128)(2,1)} %collective-permute-done.13), channel_id=1, source_target_pairs={{1,0},{2,1},{3,2},{4,3},{5,4},{6,5},{7,6},{8,7},{9,8},{10,9},{11,1... | collective-permute-start | bytes 147464 | tf_op jit(solution)/shard_map/ppermute | solution.py:25
  236.4 11.8 %collective-permute-start.15 = (bf16[480,256]{1,0:T(8,128)(2,1)S(1)}, bf16[480,256]{1,0:T(8,128)(2,1)S(1)}, u32[]{:S(2)}, u32[]{:S(2)}) collective-permute-start(bf16[480,256]{1,0:T(8,128)(2,1)S(1)} %select_convert_fusion), channel_id=1, source_target_pairs={{0,16},{16,0},{32,48},{48,32},{64,80},{80,64},{96,112},{112,96},{1... | collective-permute-start | bytes 737288 | tf_op jit(solution)/shard_map/ppermute | solution.py:52
  321.4 24.2 %all-to-all-start.1 = ((bf16[4,16,16,96]{3,2,1,0:T(8,128)(2,1)}), bf16[4,16,16,96]{3,2,1,0:T(8,128)(2,1)S(1)}, u32[]{:S(2)}, u32[]{:S(2)}) async-start(bf16[4,16,16,96]{3,2,1,0:T(8,128)(2,1)} %broadcast_in_dim.71), calls=%async_computation.1 | async-start | bytes 524288 | tf_op jit(solution)/shard_map/all_to_all | solution.py:62
  340.7 99.6 %collective-permute-start.17 = (f32[48,256]{1,0:T(8,128)S(1)}, f32[48,256]{1,0:T(8,128)}, u32[]{:S(2)}, u32[]{:S(2)}) collective-permute-start(f32[48,256]{1,0:T(8,128)S(1)} %fusion.57), channel_id=1, source_target_pairs={{0,16},{16,0},{32,48},{48,32},{64,80},{80,64},{96,112},{112,96},{1... | collective-permute-start | bytes 147464 | tf_op jit(solution)/shard_map/ppermute | solution.py:52
  356.8 10.5 %all-to-all-start.2 = ((bf16[8,2,32,96]{3,2,1,0:T(8,128)(2,1)}), bf16[8,2,32,96]{3,2,1,0:T(8,128)(2,1)S(1)}, u32[]{:S(2)}, u32[]{:S(2)}) async-start(bf16[8,2,32,96]{3,2,1,0:T(8,128)(2,1)} %bitcast.73), calls=%async_computation.2 | async-start | bytes 262144 | tf_op jit(solution)/shard_map/all_to_all | solution.py:62
  368.0 9.4 %all-to-all-start.3 = ((bf16[8,2,32,96]{3,2,1,0:T(8,128)(2,1)}), bf16[8,2,32,96]{3,2,1,0:T(8,128)(2,1)S(1)}, u32[]{:S(2)}, u32[]{:S(2)}) async-start(bf16[8,2,32,96]{3,2,1,0:T(8,128)(2,1)} %broadcast_in_dim.78), calls=%async_computation.3 | async-start | bytes 262144 | tf_op jit(solution)/shard_map/all_to_all | solution.py:62
  380.7 10.4 %all-to-all-start.4 = ((bf16[16,1,32,96]{3,2,1,0:T(8,128)(2,1)}), bf16[16,1,32,96]{3,2,1,0:T(8,128)(2,1)S(1)}, u32[]{:S(2)}, u32[]{:S(2)}) async-start(bf16[16,1,32,96]{3,2,1,0:T(8,128)(2,1)} %fusion.36), calls=%async_computation.4 | async-start | bytes 262144 | tf_op jit(solution)/shard_map/all_to_all | solution.py:62
  391.8 10.2 %all-to-all-start.5 = ((bf16[16,1,32,96]{3,2,1,0:T(8,128)(2,1)}), bf16[16,1,32,96]{3,2,1,0:T(8,128)(2,1)S(1)}, u32[]{:S(2)}, u32[]{:S(2)}) async-start(bf16[16,1,32,96]{3,2,1,0:T(8,128)(2,1)} %broadcast_in_dim.81), calls=%async_computation.5 | async-start | bytes 262144 | tf_op jit(solution)/shard_map/all_to_all | solution.py:62
  405.5 13.0 %all-to-all-start.6 = ((bf16[32,2,768]{2,1,0:T(2,128)(2,1)}), bf16[32,2,768]{2,1,0:T(2,128)(2,1)S(1)}, u32[]{:S(2)}, u32[]{:S(2)}) async-start(bf16[32,2,768]{2,1,0:T(2,128)(2,1)} %reshape.304), calls=%async_computation.6 | async-start | bytes 196608 | tf_op jit(solution)/shard_map/all_to_all | solution.py:62
  419.8 11.5 %all-to-all-start.7 = ((bf16[32,2,768]{2,1,0:T(2,128)(2,1)}), bf16[32,2,768]{2,1,0:T(2,128)(2,1)S(1)}, u32[]{:S(2)}, u32[]{:S(2)}) async-start(bf16[32,2,768]{2,1,0:T(2,128)(2,1)} %reshape.306), calls=%async_computation.7 | async-start | bytes 196608 | tf_op jit(solution)/shard_map/all_to_all | solution.py:62
  434.0 16.4 %all-to-all-start.8 = ((bf16[16,2,720]{2,1,0:T(2,128)(2,1)}), bf16[16,2,720]{2,1,0:T(2,128)(2,1)S(1)}, u32[]{:S(2)}, u32[]{:S(2)}) async-start(bf16[16,2,720]{2,1,0:T(2,128)(2,1)} %reshape.308), calls=%async_computation.8 | async-start | bytes 98304 | tf_op jit(solution)/shard_map/all_to_all | solution.py:229
  (20 other events, 765.9 us)
Sparse Core Ops, SparseCore 0:
  9.4 76.0 all-gather.5
  87.5 115.0 all-gather.7
